TPU v7x, 32 devices: a whole 2x2x4 slice. The times are simulated.
32 devices in a mesh: prow: 4 (over x, core), pcol: 8 (over z, y).
Axes of the slice: x: 2, y: 2, z: 4, core: 2. Of those that a mesh axis runs over, the one named last changes fastest.
Arguments:
- coords: int32 [3, 8192], P(None, ('prow', 'pcol')), may hold values from 0 to 1023
- block_map: int32 [64], replicated, may hold values from 0 to 63, each once
- pattern: int32 [2, 64], replicated, may hold values 0 or 1
Outputs:
- factor: float32 [16, 4, 128, 8, 8, 128], P(None, 'prow', None, None, 'pcol')
Inputs may be any that keep to these rules, and one draw needn't show every extreme that they name: `block_map`: every block number appears once.
All inputs are finite; a program needn't handle non-finite values.
Results may differ from a plain program's by a relative error of at most 0.0001.
Values sent between devices are 32-bit elements; how exact they have to be, the bound alone decides.
No kernel may reach another device: no remote copies, remote signals or barrier semaphores. Data moves between devices by JAX's collectives and lax.ppermute only.
A program may use at most 128 MiB of HBM per device.

v0:
```python
import jax
import jax.numpy as jnp
from jax import lax
from jax.sharding import PartitionSpec as P

BLOCK = 128
SNODE_BLOCKS = 4
PANELS = 2
spread_factor = 89.0
scale_gain = 8.0


def spread_2(value, axis, source):
    kept = jnp.where(lax.axis_index(axis) == source, value, 0).astype(value.dtype)
    return lax.psum(kept, axis)


def lookup(table, index):
    spots = jnp.arange(table.shape[-1], dtype=jnp.int32)
    return jnp.sum(jnp.where(index[..., None] == spots, table, 0), axis=-1)


def member(panel_at, ids, pattern):
    first = panel_at * SNODE_BLOCKS
    stop = first + SNODE_BLOCKS
    value = lookup(pattern[panel_at], ids)
    own = (ids >= first) & (ids < stop)
    before = ids < first
    return jnp.where(own, 1, jnp.where(before, 0, value)).astype(jnp.float32)


def block_mask(row_ids, col_ids, pattern):
    weight = (row_ids[:, None] == col_ids[None, :]).astype(jnp.float32)
    for panel_at in range(PANELS):
        row_in = member(panel_at, row_ids, pattern)
        col_in = member(panel_at, col_ids, pattern)
        weight = weight + row_in[:, None] * col_in[None, :]
    return weight


def wendland(dist_sq, radius):
    ratio = jnp.sqrt(dist_sq) / radius
    rest = jnp.maximum(1.0 - ratio, 0.0)
    rest_sq = rest * rest
    return rest_sq * rest_sq * rest_sq * ((35.0 * ratio + 18.0) * ratio + 3.0) * (1.0 / 3.0)


def local(coords, block_map, pattern):
    rows_n = lax.axis_size("prow")
    cols_n = lax.axis_size("pcol")
    prow_at = lax.axis_index("prow")
    pcol_at = lax.axis_index("pcol")
    nblocks = block_map.shape[0]
    row_count = nblocks // rows_n
    col_count = nblocks // cols_n
    front = nblocks * BLOCK
    width = SNODE_BLOCKS * BLOCK
    radius = (spread_factor / front) ** (1.0 / 3.0)
    all_points = lax.all_gather(coords, ("prow", "pcol"), axis=1, tiled=True)
    inverse = (
        jnp.zeros((nblocks,), jnp.int32).at[block_map].set(jnp.arange(nblocks, dtype=jnp.int32))
    )
    placed = all_points.reshape(3, nblocks, BLOCK)[:, inverse, :]
    points = placed.astype(jnp.float32) * (1.0 / 1024.0)
    row_pts = lax.dynamic_index_in_dim(
        points.reshape(3, row_count, rows_n, BLOCK), prow_at, 2, keepdims=False
    )
    col_pts = lax.dynamic_index_in_dim(
        points.reshape(3, col_count, cols_n, BLOCK), pcol_at, 2, keepdims=False
    )
    row_ids = jnp.arange(row_count, dtype=jnp.int32) * rows_n + prow_at
    col_ids = jnp.arange(col_count, dtype=jnp.int32) * cols_n + pcol_at
    dist = (row_pts[0][:, :, None, None] - col_pts[0][None, None, :, :]) ** 2
    dist = dist + (row_pts[1][:, :, None, None] - col_pts[1][None, None, :, :]) ** 2
    dist = dist + (row_pts[2][:, :, None, None] - col_pts[2][None, None, :, :]) ** 2
    mask = block_mask(row_ids, col_ids, pattern)
    coupling = wendland(dist, radius) * mask[:, None, :, None]
    row_part = jnp.sum(coupling, axis=(2, 3))
    col_part = jnp.sum(coupling, axis=(0, 1))
    row_total = lax.psum(row_part, "pcol")
    col_total = lax.psum(col_part, "prow")
    row_scale = scale_gain * lax.rsqrt(1.0 + row_total)
    col_scale = scale_gain * lax.rsqrt(1.0 + col_total)
    same_block = (row_ids[:, None] == col_ids[None, :])[:, None, :, None]
    same_cell = (jnp.arange(BLOCK)[:, None] == jnp.arange(BLOCK)[None, :])[None, :, None, :]
    matrix = coupling * row_scale[:, :, None, None] * col_scale[None, None, :, :]
    matrix = matrix + (same_block & same_cell).astype(jnp.float32)
    for panel_at in range(PANELS):
        first = panel_at * SNODE_BLOCKS
        stop = first + SNODE_BLOCKS
        owner_block = first // cols_n
        column_piece = matrix[:, :, owner_block, :]
        spread = lax.all_gather(column_piece, "pcol", axis=2, tiled=True)
        begin = first % cols_n * BLOCK
        panel = spread[:, :, begin : begin + width]
        offset = (prow_at - first) % rows_n
        valid = (offset < SNODE_BLOCKS).astype(jnp.float32)
        local_row = jnp.minimum((first + offset) // rows_n, row_count - 1)
        piece = lax.dynamic_index_in_dim(panel, local_row, 0, keepdims=False) * valid
        stacked = lax.all_gather(piece, "prow", axis=0, tiled=True)
        diagonal = jnp.concatenate(
            [
                stacked[(first + step) % rows_n * BLOCK : ((first + step) % rows_n + 1) * BLOCK]
                for step in range(SNODE_BLOCKS)
            ],
            axis=0,
        )
        lower = jnp.linalg.cholesky(diagonal)
        flat = panel.reshape(row_count * BLOCK, width)
        solved = lax.linalg.triangular_solve(
            lower, flat, left_side=False, lower=True, transpose_a=True
        )
        factor_rows = (
            solved.reshape(row_count, BLOCK, width)
            * (row_ids >= first).astype(jnp.float32)[:, None, None]
        )
        trail_rows = factor_rows * (row_ids >= stop).astype(jnp.float32)[:, None, None]
        chosen = factor_rows[col_ids // rows_n]
        root = pcol_at % rows_n
        col_rows = spread_2(chosen, "prow", root)
        col_trail = col_rows * (col_ids >= stop).astype(jnp.float32)[:, None, None]
        update = jnp.einsum("aik,cjk->aicj", trail_rows, col_trail, precision=lax.Precision.HIGHEST)
        matrix = matrix - update
        in_panel = (col_ids >= first) & (col_ids < stop)
        which = jnp.clip(col_ids - first, 0, SNODE_BLOCKS - 1)
        taken = jnp.take(factor_rows.reshape(row_count, BLOCK, SNODE_BLOCKS, BLOCK), which, axis=2)
        matrix = jnp.where(in_panel[None, None, :, None], taken, matrix)
        row_in = (row_ids >= first) & (row_ids < stop)
        upper = row_in[:, None] & (col_ids >= stop)[None, :]
        matrix = jnp.where(upper[:, None, :, None], 0.0, matrix)
    return matrix.reshape(row_count, 1, BLOCK, col_count, 1, BLOCK)


def solution(mesh):
    placed = (P(None, ("prow", "pcol")), P(), P())
    return jax.shard_map(
        local,
        mesh=mesh,
        in_specs=placed,
        out_specs=P(None, "prow", None, None, "pcol", None),
        check_vma=False,
    )
```

profile of v0, /device:TPU:0, one launch (start us, length us, event | category | flops | bytes accessed | tf_op | source)
XLA Modules:
  0.0 940.7 jit_solution(6668163431641681821)
XLA Ops:
  8.0 70.7 %all_gather.15 = s32[3,8192]{1,0:T(4,128)S(1)} all-gather(s32[3,256]{1,0:T(4,128)} %param.8), channel_id=1, replica_groups=mesh['prow'=4,'pcol'=8] {'prow','pcol'}, dimensions={1}, use_global_device_ids=true | all-gather | bytes 101376 | tf_op jit(solution)/shard_map/all_gather | solution.py:59
  80.8 8.7 fusion.12
  89.5 17.4 %psum.28 = f32[16,128]{1,0:T(8,128)S(1)} all-reduce(f32[16,128]{1,0:T(8,128)S(1)} %get-tuple-element.24), channel_id=1, replica_groups=mesh['prow'=4,'pcol'=8] {'pcol'}, use_global_device_ids=true, to_apply=%region_6.7 | all-reduce | flops 2048 | bytes 16384 | tf_op jit(solution)/shard_map/psum | solution.py:80
  106.9 6.0 psum.29
  112.9 9.8 %convert_add_fusion = f32[16,128,8,128]{1,3,0,2:T(8,128)S(1)} fusion(f32[8,128]{1,0:T(8,128)S(1)} %rsqrt_multiply_fusion.1, f32[16,128]{1,0:T(8,128)S(1)} %rsqrt_multiply_fusion, f32[16,8]{0,1:T(8,128)S(1)} %add_multiply_fusion, f32[8,128]{1,0:T(8,128)S(1)} %bitcast.216, f32[16,128]{1,0:T(8,128)S(1)} %bitcast.207, f32[8,128]{1,0:T(8,128)S(1)} %bitcast.213, ...), kind=kLoop, calls=%fused_computation.18 | loop fusion | flops 52428800 | bytes 8454784 | tf_op jit(solution)/shard_map/add | solution.py:87
  123.9 122.2 %all-gather.9.cloned.1.call-done = f32[16,128,1,1024]{1,3,0,2:T(8,128)} async-done(((f32[16,128,1,128]{1,3,0,2:T(8,128)}), f32[16,128,1,1024]{1,3,0,2:T(8,128)}) %all-gather.9.cloned.1.call-update) | async-done | bytes 8388624 | tf_op jit(solution)/shard_map/all_gather | solution.py:93
  246.2 2.5 slice.214
  248.7 2.0 copy-done
  251.6 5.5 copy.29
  257.1 9.5 %all-gather.11.cloned.1.call-done = f32[1,512,512]{1,2,0:T(8,128)} async-done(((f32[1,128,512]{1,2,0:T(8,128)}), f32[1,512,512]{1,2,0:T(8,128)}) %all-gather.11.cloned.1.call-update) | async-done | bytes 1048592 | tf_op jit(solution)/shard_map/all_gather | solution.py:100
  269.6 11.7 %cholesky.286 = f32[128,128]{1,0:T(8,128)S(1)} custom-call(f32[128,128]{1,0:T(8,128)S(1)} %cholesky.426), custom_call_target="Cholesky" | custom-call | tf_op jit(solution)/shard_map/jit(cholesky)/cholesky | solution.py:108
  281.5 9.8 %custom-call.27 = f32[1,128,128]{1,2,0:T(8,128)S(1)} custom-call(f32[1,128,128]{2,1,0:T(8,128)S(1)} %get-tuple-element.79), custom_call_target="InvertDiagBlocksLowerTriangular" | custom-call | tf_op jit(solution)/shard_map/jit(cholesky)/cholesky | solution.py:108
  292.0 11.7 %cholesky.305 = f32[128,128]{1,0:T(8,128)S(1)} custom-call(f32[128,128]{1,0:T(8,128)S(1)} %cholesky.430), custom_call_target="Cholesky" | custom-call | tf_op jit(solution)/shard_map/jit(cholesky)/cholesky | solution.py:108
  305.0 10.2 %custom-call.28 = f32[1,128,128]{1,2,0:T(8,128)S(1)} custom-call(f32[1,128,128]{2,1,0:T(8,128)S(1)} %get-tuple-element.76), custom_call_target="InvertDiagBlocksLowerTriangular" | custom-call | tf_op jit(solution)/shard_map/jit(cholesky)/cholesky | solution.py:108
  315.9 11.7 %cholesky.326 = f32[128,128]{1,0:T(8,128)S(1)} custom-call(f32[128,128]{1,0:T(8,128)S(1)} %cholesky.435), custom_call_target="Cholesky" | custom-call | tf_op jit(solution)/shard_map/jit(cholesky)/cholesky | solution.py:108
  328.3 9.8 %custom-call.29 = f32[1,128,128]{1,2,0:T(8,128)S(1)} custom-call(f32[1,128,128]{2,1,0:T(8,128)S(1)} %get-tuple-element.73), custom_call_target="InvertDiagBlocksLowerTriangular" | custom-call | tf_op jit(solution)/shard_map/jit(cholesky)/cholesky | solution.py:108
  338.7 11.7 %cholesky.343 = f32[128,128]{1,0:T(8,128)S(1)} custom-call(f32[128,128]{1,0:T(8,128)S(1)} %convolution_subtract_fusion.9), custom_call_target="Cholesky" | custom-call | tf_op jit(solution)/shard_map/jit(cholesky)/cholesky | solution.py:108
  354.1 7.9 while.4
  362.0 39.3 %custom-call.30 = f32[4,128,128]{1,2,0:T(8,128)S(1)} custom-call(f32[4,128,128]{2,1,0:T(8,128)S(1)} %get-tuple-element.22), custom_call_target="InvertDiagBlocksLowerTriangular" | custom-call | tf_op jit(solution)/shard_map/triangular_solve/custom-call.3 | solution.py:110
  401.3 2.3 fusion.53
  403.6 3.0 convolution_subtract_fusion.3
  407.7 4.9 convolution_subtract_fusion.1
  413.7 6.8 fusion.28
  421.6 4.4 pad_maximum_fusion
  425.9 5.3 copy.45
  431.3 4.8 broadcast_multiply_fusion.2
  436.1 2.9 gather_fusion.1
  440.9 5.1 copy.47
  446.0 5.3 copy.30
  451.3 4.9 broadcast_multiply_fusion.3
  456.2 6.7 gather_fusion.3
  462.9 9.2 copy.31
  472.0 20.2 %all-reduce.4.cloned.1.call-done = f32[8,128,512]{2,1,0:T(8,128)} async-done(((f32[8,128,512]{2,1,0:T(8,128)}), f32[8,128,512]{2,1,0:T(8,128)}) %all-reduce.4.cloned.1.call-update) | async-done | bytes 2097168 | tf_op jit(solution)/shard_map/psum | solution.py:15
  492.2 26.2 %fusion.4 = f32[16,128,8,128]{1,3,0,2:T(8,128)S(1)} fusion(f32[8,16,128,128]{2,3,1,0:T(8,128)} %copy.31, pred[8]{0:T(512)(128)(4,1)S(1)} %get-tuple-element.88, pred[8]{0:T(512)(128)(4,1)S(1)} %get-tuple-element.89, pred[16,8]{0,1:T(8,128)(4,1)S(1)} %broadcast_and_fusion, f32[8,128,512]{2,1,0:T(8,128)} %all-reduce.4.cloned.1.call-done, ...), kind=kOutput, calls=%fused_computation.17 | convolution fusion | flops 12947292160 | bytes 23135088 | tf_op jit(solution)/shard_map/aik,cjk->aicj/dot_general | solution.py:122
  518.5 3.2 copy-done.2
  522.9 124.6 %all-gather.13.cloned.1.call-done = f32[16,128,1,1024]{1,3,0,2:T(8,128)} async-done(((f32[16,128,1,128]{1,3,0,2:T(8,128)}), f32[16,128,1,1024]{1,3,0,2:T(8,128)}) %all-gather.13.cloned.1.call-update) | async-done | bytes 8388624 | tf_op jit(solution)/shard_map/all_gather | solution.py:93
  647.5 2.5 slice.227
  652.8 5.5 copy.35
  658.3 9.6 %all-gather.15.cloned.1.call-done = f32[1,512,512]{1,2,0:T(8,128)} async-done(((f32[1,128,512]{1,2,0:T(8,128)}), f32[1,512,512]{1,2,0:T(8,128)}) %all-gather.15.cloned.1.call-update) | async-done | bytes 1048592 | tf_op jit(solution)/shard_map/all_gather | solution.py:100
  670.9 11.7 %cholesky.358 = f32[128,128]{1,0:T(8,128)S(1)} custom-call(f32[128,128]{1,0:T(8,128)S(1)} %cholesky.439), custom_call_target="Cholesky" | custom-call | tf_op jit(solution)/shard_map/jit(cholesky)/cholesky | solution.py:108
  682.8 9.8 %custom-call.31 = f32[1,128,128]{1,2,0:T(8,128)S(1)} custom-call(f32[1,128,128]{2,1,0:T(8,128)S(1)} %get-tuple-element.69), custom_call_target="InvertDiagBlocksLowerTriangular" | custom-call | tf_op jit(solution)/shard_map/jit(cholesky)/cholesky | solution.py:108
  693.3 11.7 %cholesky.377 = f32[128,128]{1,0:T(8,128)S(1)} custom-call(f32[128,128]{1,0:T(8,128)S(1)} %cholesky.443), custom_call_target="Cholesky" | custom-call | tf_op jit(solution)/shard_map/jit(cholesky)/cholesky | solution.py:108
  706.3 10.2 %custom-call.32 = f32[1,128,128]{1,2,0:T(8,128)S(1)} custom-call(f32[1,128,128]{2,1,0:T(8,128)S(1)} %get-tuple-element.66), custom_call_target="InvertDiagBlocksLowerTriangular" | custom-call | tf_op jit(solution)/shard_map/jit(cholesky)/cholesky | solution.py:108
  717.2 11.7 %cholesky.398 = f32[128,128]{1,0:T(8,128)S(1)} custom-call(f32[128,128]{1,0:T(8,128)S(1)} %cholesky.448), custom_call_target="Cholesky" | custom-call | tf_op jit(solution)/shard_map/jit(cholesky)/cholesky | solution.py:108
  729.6 9.8 %custom-call.33 = f32[1,128,128]{1,2,0:T(8,128)S(1)} custom-call(f32[1,128,128]{2,1,0:T(8,128)S(1)} %get-tuple-element.63), custom_call_target="InvertDiagBlocksLowerTriangular" | custom-call | tf_op jit(solution)/shard_map/jit(cholesky)/cholesky | solution.py:108
  740.1 11.7 %cholesky.415 = f32[128,128]{1,0:T(8,128)S(1)} custom-call(f32[128,128]{1,0:T(8,128)S(1)} %convolution_subtract_fusion.8), custom_call_target="Cholesky" | custom-call | tf_op jit(solution)/shard_map/jit(cholesky)/cholesky | solution.py:108
  755.4 7.9 while.5
  763.3 39.3 %custom-call.34 = f32[4,128,128]{1,2,0:T(8,128)S(1)} custom-call(f32[4,128,128]{2,1,0:T(8,128)S(1)} %get-tuple-element.23), custom_call_target="InvertDiagBlocksLowerTriangular" | custom-call | tf_op jit(solution)/shard_map/triangular_solve/custom-call.3 | solution.py:110
  802.7 2.3 fusion.51
  805.0 3.0 convolution_subtract_fusion.2
  809.1 4.9 convolution_subtract_fusion
  815.1 6.8 fusion.25
  822.9 4.4 pad_maximum_fusion.1
  827.3 5.4 copy.46
  832.7 4.8 broadcast_multiply_fusion.1
  837.5 2.9 gather_fusion.2
  842.2 5.1 copy.48
  847.3 5.3 copy.36
  852.6 4.9 broadcast_multiply_fusion
  857.6 6.7 gather_fusion.4
  864.3 9.2 copy.37
  873.5 20.2 %all-reduce.6.cloned.1.call-done = f32[8,128,512]{2,1,0:T(8,128)} async-done(((f32[8,128,512]{2,1,0:T(8,128)}), f32[8,128,512]{2,1,0:T(8,128)}) %all-reduce.6.cloned.1.call-update) | async-done | bytes 2097168 | tf_op jit(solution)/shard_map/psum | solution.py:15
  893.6 19.5 %fusion.3 = f32[16,1,128,8,1,128]{2,5,0,3,4,1:T(8,128)} fusion(f32[8,16,128,128]{2,3,1,0:T(8,128)} %copy.37, f32[16,128,8,128]{1,3,0,2:T(8,128)} %copy-done.2, pred[8]{0:T(512)(128)(4,1)S(1)} %get-tuple-element.94, pred[8]{0:T(512)(128)(4,1)S(1)} %get-tuple-element.95, pred[16,8]{0,1:T(8,128)(4,1)S(1)} %broadcast_and_fusion.1, ...), kind=kOutput, calls=%fused_computation.15 | convolution fusion | flops 12894863360 | bytes 31457520 | tf_op jit(solution)/shard_map/aik,cjk->aicj/dot_general | solution.py:122
  913.1 20.5 %copy.40 = f32[16,1,128,8,1,128]{5,4,3,2,1,0:T(1,128)} copy(f32[16,1,128,8,1,128]{2,5,0,3,4,1:T(8,128)} %fusion.3) | data formatting | bytes 16777216 | tf_op jit(solution)/shard_map/reshape | solution.py:131
  (135 shorter events, 51.6 us)
Async XLA Ops:
  6.5 239.6 %all-gather.9.cloned.1.call-start = ((), (), s32[]{:S(2)}) async-start(), calls=%async_computation.2 | async-start | bytes 9437184 | tf_op jit(solution)/shard_map/all_gather | solution.py:93
  123.8 142.7 %all-gather.11.cloned.1.call-start = ((), (), s32[]{:S(2)}) async-start(), calls=%async_computation.3 | async-start | bytes 1310720 | tf_op jit(solution)/shard_map/all_gather | solution.py:100
  248.6 2.0 copy-start
  251.4 240.8 %all-reduce.4.cloned.1.call-start = ((), (), s32[]{:S(2)}) async-start(), calls=%async_computation | async-start | bytes 4194304 | tf_op jit(solution)/shard_map/psum | solution.py:15
  440.7 206.8 %all-gather.13.cloned.1.call-start = ((), (), s32[]{:S(2)}) async-start(), calls=%async_computation.4 | async-start | bytes 9437184 | tf_op jit(solution)/shard_map/all_gather | solution.py:93
  518.5 3.2 copy-start.2
  522.8 145.1 %all-gather.15.cloned.1.call-start = ((), (), s32[]{:S(2)}) async-start(), calls=%async_computation.5 | async-start | bytes 1310720 | tf_op jit(solution)/shard_map/all_gather | solution.py:100
  650.0 2.0 copy-start.1
  652.7 240.9 %all-reduce.6.cloned.1.call-start = ((), (), s32[]{:S(2)}) async-start(), calls=%async_computation.1 | async-start | bytes 4194304 | tf_op jit(solution)/shard_map/psum | solution.py:15
Sparse Core Ops, SparseCore 0:
  124.0 122.1 all-gather.8
  251.5 14.9 all-gather.10
  440.8 51.3 all-reduce.3
  522.9 124.5 all-gather.12
  652.8 14.9 all-gather.14
  842.2 51.3 all-reduce.5
where the time goes:
time: 950 us; the launch traced here: 941 us
  waiting for transfers between devices  306 us (32%)
  other arithmetic  294 us (31%)
  local copies, waits for them, and re-layouts  136 us (14%)
  blocking collectives  94.1 us (10%)
  matrix products  89.9 us (9%)
  between operations  19.6 us (2%)
    all_gather x2, waiting for transfers between devices, local(): spread = lax.all_gather(column_piece, 'pcol', axis=2, tiled=True)  247 us
    another operation x30, other arithmetic, local(): lower = jnp.linalg.cholesky(diagonal)  159 us
    another operation x7, other arithmetic, local(): lax.linalg.triangular_solve(lower, flat, left_side=False, lower=True, tra...  88 us
    all_gather x1, blocking collectives, local(): all_points = lax.all_gather(coords, ('prow', 'pcol'), axis=1, tiled=True)  70.7 us
    dot_general x2, matrix products, local(): jnp.einsum('aik,cjk->aicj', trail_rows, col_trail, precision=lax.Precisio...  45.7 us
    another operation x14, matrix products, local(): lax.linalg.triangular_solve(lower, flat, left_side=False, lower=True, tra...  40.5 us
    psum x2, waiting for transfers between devices, spread_2(): return lax.psum(kept, axis)  40.3 us
    gather x4, local copies, waits for them, and re-layouts, local(): jnp.take(factor_rows.reshape(row_count, BLOCK, SNODE_BLOCKS, BLOCK), whic...  31.8 us
  transfers between devices with their start and end apart: 6, of which 6 were waited for; matrix products, arithmetic and copies ran while one was open for 8% of the time, Pallas kernels for 0%

commit v1 on v0

--- a/solution.py
+++ b/solution.py
@@ -90,7 +90,25 @@
         stop = first + SNODE_BLOCKS
         owner_block = first // cols_n
         column_piece = matrix[:, :, owner_block, :]
-        spread = lax.all_gather(column_piece, "pcol", axis=2, tiled=True)
+        ways, here, step_2 = (lax.axis_size("pcol"), lax.axis_index("pcol"), column_piece.shape[2])
+        dims = [n * ways if d == 2 else n for d, n in enumerate(column_piece.shape)]
+        full = lax.dynamic_update_slice_in_dim(
+            jnp.zeros(dims, column_piece.dtype), column_piece, here * step_2, axis=2
+        )
+        going_up = going_down = column_piece
+        for far in range(1, ways // 2 + 1):
+            going_up = lax.ppermute(going_up, "pcol", [(d, (d + 1) % ways) for d in range(ways)])
+            full = lax.dynamic_update_slice_in_dim(
+                full, going_up, (here - far) % ways * step_2, axis=2
+            )
+            if 2 * far < ways:
+                going_down = lax.ppermute(
+                    going_down, "pcol", [(d, (d - 1) % ways) for d in range(ways)]
+                )
+                full = lax.dynamic_update_slice_in_dim(
+                    full, going_down, (here + far) % ways * step_2, axis=2
+                )
+        spread = full
         begin = first % cols_n * BLOCK
         panel = spread[:, :, begin : begin + width]
         offset = (prow_at - first) % rows_n

time: 950 us -> 1030 us (1.084)
  waiting for transfers between devices: 306 us -> 342 us
  starting transfers between devices: 0.21 us -> 34.7 us
    ppermute x0 -> x14, waiting for transfers between devices: none -> 284 us  [the longest x8 284 us: local(): lax.ppermute(going_up, 'pcol', [(d, (d + 1) % ways) for d in range(ways)])]
    all_gather x2 -> x0, waiting for transfers between devices: 247 us -> none  [local(): spread = lax.all_gather(column_piece, 'pcol', axis=2, tiled=True)]
    ppermute x0 -> x14, starting transfers between devices: none -> 34.6 us  [the longest x8 18.5 us: local(): lax.ppermute(going_up, 'pcol', [(d, (d + 1) % ways) for d in range(ways)])]
    dynamic_update_slice x0 -> x16, local copies, waits for them, and re-layouts: none -> 11.2 us  [the longest x6 5.41 us: local(): lax.dynamic_update_slice_in_dim(full, going_down, (here + far) % ways * s...]
    unnamed x8 -> x14, local copies, waits for them, and re-layouts: 17.5 us -> 21 us
  transfers between devices with their start and end apart: 6 -> 18, of which waited for: 6 -> 12; matrix products, arithmetic and copies ran while one was open for 8% -> 8% of each run, Pallas kernels for 0% -> 0%
where the time goes in v1:
time: 1030 us; the launch traced here: 1020 us
  waiting for transfers between devices  342 us (33%)
  other arithmetic  294 us (29%)
  local copies, waits for them, and re-layouts  146 us (14%)
  blocking collectives  94.1 us (9%)
  matrix products  85.6 us (8%)
  starting transfers between devices  34.7 us (3%)
  between operations  19.5 us (2%)
    ppermute x8, waiting for transfers between devices, local(): lax.ppermute(going_up, 'pcol', [(d, (d + 1) % ways) for d in range(ways)])  284 us
    another operation x30, other arithmetic, local(): lower = jnp.linalg.cholesky(diagonal)  159 us
    another operation x7, other arithmetic, local(): lax.linalg.triangular_solve(lower, flat, left_side=False, lower=True, tra...  87.8 us
    all_gather x1, blocking collectives, local(): all_points = lax.all_gather(coords, ('prow', 'pcol'), axis=1, tiled=True)  70.7 us
    dot_general x2, matrix products, local(): jnp.einsum('aik,cjk->aicj', trail_rows, col_trail, precision=lax.Precisio...  45.7 us
    psum x2, waiting for transfers between devices, spread_2(): return lax.psum(kept, axis)  40.6 us
    another operation x14, matrix products, local(): lax.linalg.triangular_solve(lower, flat, left_side=False, lower=True, tra...  36.1 us
    gather x4, local copies, waits for them, and re-layouts, local(): jnp.take(factor_rows.reshape(row_count, BLOCK, SNODE_BLOCKS, BLOCK), whic...  31.6 us
  transfers between devices with their start and end apart: 18, of which 12 were waited for; matrix products, arithmetic and copies ran while one was open for 8% of the time, Pallas kernels for 0%

profile of v1, /device:TPU:0, one launch (start us, length us, event | category | flops | bytes accessed | tf_op | source)
XLA Modules:
  0.0 1015.9 jit_solution(16663552562091835902)
XLA Ops:
  8.0 70.7 %all_gather.9 = s32[3,8192]{1,0:T(4,128)S(1)} all-gather(s32[3,256]{1,0:T(4,128)} %param.8), channel_id=1, replica_groups=mesh['prow'=4,'pcol'=8] {'prow','pcol'}, dimensions={1}, use_global_device_ids=true | all-gather | bytes 101376 | tf_op jit(solution)/shard_map/all_gather | solution.py:59
  80.8 8.7 fusion.12
  89.5 17.4 %psum.28 = f32[16,128]{1,0:T(8,128)S(1)} all-reduce(f32[16,128]{1,0:T(8,128)S(1)} %get-tuple-element.24), channel_id=1, replica_groups=mesh['prow'=4,'pcol'=8] {'pcol'}, use_global_device_ids=true, to_apply=%region_6.7 | all-reduce | flops 2048 | bytes 16384 | tf_op jit(solution)/shard_map/psum | solution.py:80
  106.9 6.0 psum.29
  112.9 9.8 convert_add_fusion
  122.8 3.4 copy-done.4
  131.0 41.9 %collective-permute-done = f32[16,128,128]{1,2,0:T(8,128)S(1)} collective-permute-done((f32[16,128,128]{1,2,0:T(8,128)S(1)}, f32[16,128,128]{1,2,0:T(8,128)S(1)}, u32[]{:S(2)}, u32[]{:S(2)}) %collective-permute-start) | collective-permute-done | bytes 1048608 | tf_op jit(solution)/shard_map/ppermute | solution.py:100
  177.6 41.9 %collective-permute-done.2 = f32[16,128,128]{1,2,0:T(8,128)S(1)} collective-permute-done((f32[16,128,128]{1,2,0:T(8,128)S(1)}, f32[16,128,128]{1,2,0:T(8,128)S(1)}, u32[]{:S(2)}, u32[]{:S(2)}) %collective-permute-start.2) | collective-permute-done | bytes 1048608 | tf_op jit(solution)/shard_map/ppermute | solution.py:100
  224.2 41.9 %collective-permute-done.4 = f32[16,128,128]{1,2,0:T(8,128)} collective-permute-done((f32[16,128,128]{1,2,0:T(8,128)S(1)}, f32[16,128,128]{1,2,0:T(8,128)}, u32[]{:S(2)}, u32[]{:S(2)}) %collective-permute-start.4) | collective-permute-done | bytes 1048608 | tf_op jit(solution)/shard_map/ppermute | solution.py:100
  275.1 17.9 %collective-permute-done.6 = f32[16,128,128]{1,2,0:T(8,128)S(1)} collective-permute-done((f32[16,128,128]{1,2,0:T(8,128)}, f32[16,128,128]{1,2,0:T(8,128)S(1)}, u32[]{:S(2)}, u32[]{:S(2)}) %collective-permute-start.6) | collective-permute-done | bytes 1048608 | tf_op jit(solution)/shard_map/ppermute | solution.py:100
  296.4 5.6 copy.29
  302.0 7.6 all-gather.5.cloned.1.call-done
  312.6 11.7 %cholesky.286 = f32[128,128]{1,0:T(8,128)S(1)} custom-call(f32[128,128]{1,0:T(8,128)S(1)} %cholesky.426), custom_call_target="Cholesky" | custom-call | tf_op jit(solution)/shard_map/jit(cholesky)/cholesky | solution.py:126
  324.4 9.8 custom-call.27
  334.9 11.7 %cholesky.305 = f32[128,128]{1,0:T(8,128)S(1)} custom-call(f32[128,128]{1,0:T(8,128)S(1)} %cholesky.430), custom_call_target="Cholesky" | custom-call | tf_op jit(solution)/shard_map/jit(cholesky)/cholesky | solution.py:126
  348.0 10.2 %custom-call.28 = f32[1,128,128]{1,2,0:T(8,128)S(1)} custom-call(f32[1,128,128]{2,1,0:T(8,128)S(1)} %get-tuple-element.76), custom_call_target="InvertDiagBlocksLowerTriangular" | custom-call | tf_op jit(solution)/shard_map/jit(cholesky)/cholesky | solution.py:126
  358.9 11.7 %cholesky.326 = f32[128,128]{1,0:T(8,128)S(1)} custom-call(f32[128,128]{1,0:T(8,128)S(1)} %cholesky.435), custom_call_target="Cholesky" | custom-call | tf_op jit(solution)/shard_map/jit(cholesky)/cholesky | solution.py:126
  371.3 9.8 custom-call.29
  381.7 11.7 %cholesky.343 = f32[128,128]{1,0:T(8,128)S(1)} custom-call(f32[128,128]{1,0:T(8,128)S(1)} %convolution_subtract_fusion.5), custom_call_target="Cholesky" | custom-call | tf_op jit(solution)/shard_map/jit(cholesky)/cholesky | solution.py:126
  397.1 7.9 while.4
  405.0 39.3 %custom-call.30 = f32[4,128,128]{1,2,0:T(8,128)S(1)} custom-call(f32[4,128,128]{2,1,0:T(8,128)S(1)} %get-tuple-element.22), custom_call_target="InvertDiagBlocksLowerTriangular" | custom-call | tf_op jit(solution)/shard_map/triangular_solve/custom-call.3 | solution.py:128
  451.0 3.6 fusion.25
  455.8 5.5 fusion.13
  462.5 4.4 pad_maximum_fusion
  466.8 5.3 copy.45
  472.2 4.8 broadcast_multiply_fusion.2
  481.8 5.1 copy.47
  486.9 5.3 copy.30
  492.2 4.9 broadcast_multiply_fusion.3
  497.1 6.7 gather_fusion.3
  503.8 9.2 copy.31
  512.9 20.2 %all-reduce.4.cloned.1.call-done = f32[8,128,512]{2,1,0:T(8,128)} async-done(((f32[8,128,512]{2,1,0:T(8,128)}), f32[8,128,512]{2,1,0:T(8,128)}) %all-reduce.4.cloned.1.call-update) | async-done | bytes 2097168 | tf_op jit(solution)/shard_map/psum | solution.py:15
  533.1 26.2 %fusion.4 = f32[16,128,8,128]{1,3,0,2:T(8,128)S(1)} fusion(f32[8,16,128,128]{2,3,1,0:T(8,128)} %copy.31, pred[8]{0:T(512)(128)(4,1)S(1)} %get-tuple-element.90, pred[8]{0:T(512)(128)(4,1)S(1)} %get-tuple-element.91, pred[16,8]{0,1:T(8,128)(4,1)S(1)} %broadcast_and_fusion, f32[8,128,512]{2,1,0:T(8,128)} %all-reduce.4.cloned.1.call-done, ...), kind=kOutput, calls=%fused_computation.17 | convolution fusion | flops 12947292160 | bytes 23135088 | tf_op jit(solution)/shard_map/aik,cjk->aicj/dot_general | solution.py:140
  559.4 3.4 copy-done.5
  564.4 3.2 collective-permute-start.8
  567.7 41.4 %collective-permute-done.7 = f32[16,128,128]{1,2,0:T(8,128)S(1)} collective-permute-done((f32[16,128,128]{1,2,0:T(8,128)S(1)}, f32[16,128,128]{1,2,0:T(8,128)S(1)}, u32[]{:S(2)}, u32[]{:S(2)}) %collective-permute-start.7) | collective-permute-done | bytes 1048608 | tf_op jit(solution)/shard_map/ppermute | solution.py:100
  614.3 41.0 %collective-permute-done.9 = f32[16,128,128]{1,2,0:T(8,128)} collective-permute-done((f32[16,128,128]{1,2,0:T(8,128)S(1)}, f32[16,128,128]{1,2,0:T(8,128)}, u32[]{:S(2)}, u32[]{:S(2)}) %collective-permute-start.9) | collective-permute-done | bytes 1048608 | tf_op jit(solution)/shard_map/ppermute | solution.py:100
  660.7 40.7 %collective-permute-done.11 = f32[16,128,128]{1,2,0:T(8,128)S(1)} collective-permute-done((f32[16,128,128]{1,2,0:T(8,128)}, f32[16,128,128]{1,2,0:T(8,128)S(1)}, u32[]{:S(2)}, u32[]{:S(2)}) %collective-permute-start.11) | collective-permute-done | bytes 1048608 | tf_op jit(solution)/shard_map/ppermute | solution.py:100
  710.2 17.5 %collective-permute-done.13 = f32[16,128,128]{1,2,0:T(8,128)S(1)} collective-permute-done((f32[16,128,128]{1,2,0:T(8,128)S(1)}, f32[16,128,128]{1,2,0:T(8,128)S(1)}, u32[]{:S(2)}, u32[]{:S(2)}) %collective-permute-start.13) | collective-permute-done | bytes 1048608 | tf_op jit(solution)/shard_map/ppermute | solution.py:100
  730.9 5.5 copy.35
  736.4 9.4 all-gather.7.cloned.1.call-done
  748.8 11.7 %cholesky.358 = f32[128,128]{1,0:T(8,128)S(1)} custom-call(f32[128,128]{1,0:T(8,128)S(1)} %cholesky.439), custom_call_target="Cholesky" | custom-call | tf_op jit(solution)/shard_map/jit(cholesky)/cholesky | solution.py:126
  760.7 9.8 custom-call.31
  771.2 11.7 %cholesky.377 = f32[128,128]{1,0:T(8,128)S(1)} custom-call(f32[128,128]{1,0:T(8,128)S(1)} %cholesky.443), custom_call_target="Cholesky" | custom-call | tf_op jit(solution)/shard_map/jit(cholesky)/cholesky | solution.py:126
  784.2 10.2 %custom-call.32 = f32[1,128,128]{1,2,0:T(8,128)S(1)} custom-call(f32[1,128,128]{2,1,0:T(8,128)S(1)} %get-tuple-element.66), custom_call_target="InvertDiagBlocksLowerTriangular" | custom-call | tf_op jit(solution)/shard_map/jit(cholesky)/cholesky | solution.py:126
  795.1 11.7 %cholesky.398 = f32[128,128]{1,0:T(8,128)S(1)} custom-call(f32[128,128]{1,0:T(8,128)S(1)} %cholesky.448), custom_call_target="Cholesky" | custom-call | tf_op jit(solution)/shard_map/jit(cholesky)/cholesky | solution.py:126
  807.6 9.8 custom-call.33
  818.0 11.7 %cholesky.415 = f32[128,128]{1,0:T(8,128)S(1)} custom-call(f32[128,128]{1,0:T(8,128)S(1)} %convolution_subtract_fusion.4), custom_call_target="Cholesky" | custom-call | tf_op jit(solution)/shard_map/jit(cholesky)/cholesky | solution.py:126
  833.2 7.8 while.5
  841.0 39.3 %custom-call.34 = f32[4,128,128]{1,2,0:T(8,128)S(1)} custom-call(f32[4,128,128]{2,1,0:T(8,128)S(1)} %get-tuple-element.23), custom_call_target="InvertDiagBlocksLowerTriangular" | custom-call | tf_op jit(solution)/shard_map/triangular_solve/custom-call.3 | solution.py:128
  887.0 3.6 fusion.29
  891.8 5.5 fusion.19
  898.5 4.2 pad_maximum_fusion.1
  902.7 5.3 copy.46
  908.1 4.8 broadcast_multiply_fusion.1
  912.8 2.9 gather_fusion.2
  917.6 5.1 copy.48
  922.6 5.3 copy.36
  928.0 4.9 broadcast_multiply_fusion
  932.9 6.5 gather_fusion.4
  939.4 9.2 copy.37
  948.6 20.4 %all-reduce.6.cloned.1.call-done = f32[8,128,512]{2,1,0:T(8,128)} async-done(((f32[8,128,512]{2,1,0:T(8,128)}), f32[8,128,512]{2,1,0:T(8,128)}) %all-reduce.6.cloned.1.call-update) | async-done | bytes 2097168 | tf_op jit(solution)/shard_map/psum | solution.py:15
  969.0 19.5 %fusion.3 = f32[16,1,128,8,1,128]{2,5,0,3,4,1:T(8,128)} fusion(f32[8,16,128,128]{2,3,1,0:T(8,128)} %copy.37, f32[16,128,8,128]{1,3,0,2:T(8,128)} %copy-done.5, pred[8]{0:T(512)(128)(4,1)S(1)} %get-tuple-element.88, pred[8]{0:T(512)(128)(4,1)S(1)} %get-tuple-element.89, pred[16,8]{0,1:T(8,128)(4,1)S(1)} %broadcast_and_fusion.1, ...), kind=kOutput, calls=%fused_computation.15 | convolution fusion | flops 12894863360 | bytes 31457520 | tf_op jit(solution)/shard_map/aik,cjk->aicj/dot_general | solution.py:140
  988.4 20.5 %copy.40 = f32[16,1,128,8,1,128]{5,4,3,2,1,0:T(1,128)} copy(f32[16,1,128,8,1,128]{2,5,0,3,4,1:T(8,128)} %fusion.3) | data formatting | bytes 16777216 | tf_op jit(solution)/shard_map/reshape | solution.py:149
  (181 shorter events, 110.4 us)
Async XLA Ops:
  6.5 303.0 %all-gather.5.cloned.1.call-start = ((), (), s32[]{:S(2)}) async-start(), calls=%async_computation.2 | async-start | bytes 1310720 | tf_op jit(solution)/shard_map/all_gather | solution.py:118
  122.8 3.4 copy-start.4
  126.2 46.7 %collective-permute-start = (f32[16,128,128]{1,2,0:T(8,128)S(1)}, f32[16,128,128]{1,2,0:T(8,128)S(1)}, u32[]{:S(2)}, u32[]{:S(2)}) collective-permute-start(f32[16,128,128]{1,2,0:T(8,128)S(1)} %slice_bitcast_fusion.1), channel_id=1, source_target_pairs={{0,1},{1,2},{2,3},{3,4},{4,5},{5,6},{6,7},{7,0},{8,9},{9,10},{10,1... | collective-permute-start | bytes 3145736 | tf_op jit(solution)/shard_map/ppermute | solution.py:100
  128.2 47.1 %collective-permute-start.1 = (f32[16,128,128]{1,2,0:T(8,128)S(1)}, f32[16,128,128]{1,2,0:T(8,128)S(1)}, u32[]{:S(2)}, u32[]{:S(2)}) collective-permute-start(f32[16,128,128]{1,2,0:T(8,128)S(1)} %slice_bitcast_fusion.1), channel_id=1, source_target_pairs={{0,7},{1,0},{2,1},{3,2},{4,3},{5,4},{6,5},{7,6},{8,15},{9,8},{10,9... | collective-permute-start | bytes 3145736 | tf_op jit(solution)/shard_map/ppermute | solution.py:105
  172.9 46.6 %collective-permute-start.2 = (f32[16,128,128]{1,2,0:T(8,128)S(1)}, f32[16,128,128]{1,2,0:T(8,128)S(1)}, u32[]{:S(2)}, u32[]{:S(2)}) collective-permute-start(f32[16,128,128]{1,2,0:T(8,128)S(1)} %collective-permute-done), channel_id=1, source_target_pairs={{0,1},{1,2},{2,3},{3,4},{4,5},{5,6},{6,7},{7,0},{8,9},{9,10},{10,1... | collective-permute-start | bytes 3145736 | tf_op jit(solution)/shard_map/ppermute | solution.py:100
  175.4 46.6 %collective-permute-start.3 = (f32[16,128,128]{1,2,0:T(8,128)S(1)}, f32[16,128,128]{1,2,0:T(8,128)}, u32[]{:S(2)}, u32[]{:S(2)}) collective-permute-start(f32[16,128,128]{1,2,0:T(8,128)S(1)} %collective-permute-done.1), channel_id=1, source_target_pairs={{0,7},{1,0},{2,1},{3,2},{4,3},{5,4},{6,5},{7,6},{8,15},{9,8},{10,9... | collective-permute-start | bytes 3145736 | tf_op jit(solution)/shard_map/ppermute | solution.py:105
  219.5 46.6 %collective-permute-start.4 = (f32[16,128,128]{1,2,0:T(8,128)S(1)}, f32[16,128,128]{1,2,0:T(8,128)}, u32[]{:S(2)}, u32[]{:S(2)}) collective-permute-start(f32[16,128,128]{1,2,0:T(8,128)S(1)} %collective-permute-done.2), channel_id=1, source_target_pairs={{0,1},{1,2},{2,3},{3,4},{4,5},{5,6},{6,7},{7,0},{8,9},{9,10},{10,1... | collective-permute-start | bytes 3145736 | tf_op jit(solution)/shard_map/ppermute | solution.py:100
  222.0 51.8 %collective-permute-start.5 = (f32[16,128,128]{1,2,0:T(8,128)}, f32[16,128,128]{1,2,0:T(8,128)}, u32[]{:S(2)}, u32[]{:S(2)}) collective-permute-start(f32[16,128,128]{1,2,0:T(8,128)} %collective-permute-done.3), channel_id=1, source_target_pairs={{0,7},{1,0},{2,1},{3,2},{4,3},{5,4},{6,5},{7,6},{8,15},{9,8},{10,9... | collective-permute-start | bytes 3145736 | tf_op jit(solution)/shard_map/ppermute | solution.py:105
  266.1 26.9 %collective-permute-start.6 = (f32[16,128,128]{1,2,0:T(8,128)}, f32[16,128,128]{1,2,0:T(8,128)S(1)}, u32[]{:S(2)}, u32[]{:S(2)}) collective-permute-start(f32[16,128,128]{1,2,0:T(8,128)} %collective-permute-done.4), channel_id=1, source_target_pairs={{0,1},{1,2},{2,3},{3,4},{4,5},{5,6},{6,7},{7,0},{8,9},{9,10},{10,1... | collective-permute-start | bytes 3145736 | tf_op jit(solution)/shard_map/ppermute | solution.py:100
  293.5 2.0 copy-start
  296.3 236.9 %all-reduce.4.cloned.1.call-start = ((), (), s32[]{:S(2)}) async-start(), calls=%async_computation | async-start | bytes 4194304 | tf_op jit(solution)/shard_map/psum | solution.py:15
  444.3 10.3 %copy-start.3 = (f32[16,128,512]{2,1,0:T(8,128)S(1)}, f32[16,128,512]{2,1,0:T(8,128)}, u32[]{:S(2)}) copy-start(f32[16,128,512]{2,1,0:T(8,128)} %copy.29) | copy-start | bytes 12582916
  481.6 264.2 %all-gather.7.cloned.1.call-start = ((), (), s32[]{:S(2)}) async-start(), calls=%async_computation.3 | async-start | bytes 1310720 | tf_op jit(solution)/shard_map/all_gather | solution.py:118
  559.4 3.4 copy-start.5
  562.9 46.2 %collective-permute-start.7 = (f32[16,128,128]{1,2,0:T(8,128)S(1)}, f32[16,128,128]{1,2,0:T(8,128)S(1)}, u32[]{:S(2)}, u32[]{:S(2)}) collective-permute-start(f32[16,128,128]{1,2,0:T(8,128)S(1)} %slice_bitcast_fusion), channel_id=1, source_target_pairs={{0,1},{1,2},{2,3},{3,4},{4,5},{5,6},{6,7},{7,0},{8,9},{9,10},{10,1... | collective-permute-start | bytes 3145736 | tf_op jit(solution)/shard_map/ppermute | solution.py:100
  564.4 47.1 %collective-permute-start.8 = (f32[16,128,128]{1,2,0:T(8,128)S(1)}, f32[16,128,128]{1,2,0:T(8,128)S(1)}, u32[]{:S(2)}, u32[]{:S(2)}) collective-permute-start(f32[16,128,128]{1,2,0:T(8,128)S(1)} %slice_bitcast_fusion), channel_id=1, source_target_pairs={{0,7},{1,0},{2,1},{3,2},{4,3},{5,4},{6,5},{7,6},{8,15},{9,8},{10,9... | collective-permute-start | bytes 3145736 | tf_op jit(solution)/shard_map/ppermute | solution.py:105
  609.1 46.3 %collective-permute-start.9 = (f32[16,128,128]{1,2,0:T(8,128)S(1)}, f32[16,128,128]{1,2,0:T(8,128)}, u32[]{:S(2)}, u32[]{:S(2)}) collective-permute-start(f32[16,128,128]{1,2,0:T(8,128)S(1)} %collective-permute-done.7), channel_id=1, source_target_pairs={{0,1},{1,2},{2,3},{3,4},{4,5},{5,6},{6,7},{7,0},{8,9},{9,10},{10,1... | collective-permute-start | bytes 3145736 | tf_op jit(solution)/shard_map/ppermute | solution.py:100
  611.6 46.4 %collective-permute-start.10 = (f32[16,128,128]{1,2,0:T(8,128)S(1)}, f32[16,128,128]{1,2,0:T(8,128)}, u32[]{:S(2)}, u32[]{:S(2)}) collective-permute-start(f32[16,128,128]{1,2,0:T(8,128)S(1)} %collective-permute-done.8), channel_id=1, source_target_pairs={{0,7},{1,0},{2,1},{3,2},{4,3},{5,4},{6,5},{7,6},{8,15},{9,8},{10,9... | collective-permute-start | bytes 3145736 | tf_op jit(solution)/shard_map/ppermute | solution.py:105
  655.3 46.1 %collective-permute-start.11 = (f32[16,128,128]{1,2,0:T(8,128)}, f32[16,128,128]{1,2,0:T(8,128)S(1)}, u32[]{:S(2)}, u32[]{:S(2)}) collective-permute-start(f32[16,128,128]{1,2,0:T(8,128)} %collective-permute-done.9), channel_id=1, source_target_pairs={{0,1},{1,2},{2,3},{3,4},{4,5},{5,6},{6,7},{7,0},{8,9},{9,10},{10,1... | collective-permute-start | bytes 3145736 | tf_op jit(solution)/shard_map/ppermute | solution.py:100
  657.9 50.9 %collective-permute-start.12 = (f32[16,128,128]{1,2,0:T(8,128)}, f32[16,128,128]{1,2,0:T(8,128)}, u32[]{:S(2)}, u32[]{:S(2)}) collective-permute-start(f32[16,128,128]{1,2,0:T(8,128)} %collective-permute-done.10), channel_id=1, source_target_pairs={{0,7},{1,0},{2,1},{3,2},{4,3},{5,4},{6,5},{7,6},{8,15},{9,8},{10,9... | collective-permute-start | bytes 3145736 | tf_op jit(solution)/shard_map/ppermute | solution.py:105
  701.4 26.2 %collective-permute-start.13 = (f32[16,128,128]{1,2,0:T(8,128)S(1)}, f32[16,128,128]{1,2,0:T(8,128)S(1)}, u32[]{:S(2)}, u32[]{:S(2)}) collective-permute-start(f32[16,128,128]{1,2,0:T(8,128)S(1)} %collective-permute-done.11), channel_id=1, source_target_pairs={{0,1},{1,2},{2,3},{3,4},{4,5},{5,6},{6,7},{7,0},{8,9},{9,10},{10,1... | collective-permute-start | bytes 3145736 | tf_op jit(solution)/shard_map/ppermute | solution.py:100
  728.1 2.0 copy-start.1
  730.8 238.1 %all-reduce.6.cloned.1.call-start = ((), (), s32[]{:S(2)}) async-start(), calls=%async_computation.1 | async-start | bytes 4194304 | tf_op jit(solution)/shard_map/psum | solution.py:15
  880.4 10.3 %copy-start.2 = (f32[16,128,512]{2,1,0:T(8,128)S(1)}, f32[16,128,512]{2,1,0:T(8,128)}, u32[]{:S(2)}) copy-start(f32[16,128,512]{2,1,0:T(8,128)} %copy.35) | copy-start | bytes 12582916
Sparse Core Ops, SparseCore 0:
  296.4 13.1 all-gather.4
  481.7 51.3 all-reduce.3
  731.0 14.7 all-gather.6
  917.5 51.3 all-reduce.5
